TPU v7x, 128 devices: a whole 4x4x4 slice. The times are simulated.
128 devices in a mesh: dp: 16 (over x, z_lo, core), tensor: 8 (over z_hi, y).
Axes of the slice: x: 4, y: 4, z: 4 (z_hi: 2, z_lo: 2; z = z_hi * 2 + z_lo), core: 2. Of those that a mesh axis runs over, the one named last changes fastest.
Arguments:
- tokens: bfloat16 [8192, 2048], P('dp'), may hold values from -6 to 6
- first_gain: float32 [2048], replicated, may hold values from 0.5 to 1.5
- first_shift: float32 [2048], replicated, may hold values from -1.75 to 1.75
- query_weight: float32 [2048, 2048], P('dp', 'tensor'), may hold values from -0.125 to 0.125
- query_bias: float32 [2048], P('tensor'), may hold values from -3 to 3
- key_weight: float32 [2048, 2048], P('dp', 'tensor'), may hold values from -0.125 to 0.125
- value_weight: float32 [2048, 2048], P('dp', 'tensor'), may hold values from -0.125 to 0.125
- value_bias: float32 [2048], P('tensor'), may hold values from -3 to 3
- out_weight: float32 [2048, 2048], P('tensor', 'dp'), may hold values from -0.5 to 0.5
- out_bias: float32 [2048], replicated, may hold values from -1.75 to 1.75
- second_gain: float32 [2048], replicated, may hold values from 0.5 to 1.5
- second_shift: float32 [2048], replicated, may hold values from -1.75 to 1.75
- up_weight: float32 [2048, 8192], P('dp', 'tensor'), may hold values from -0.125 to 0.125
- up_bias: float32 [8192], P('tensor'), may hold values from -3 to 3
- down_weight: float32 [8192, 2048], P('tensor', 'dp'), may hold values from -0.0625 to 0.0625
- down_bias: float32 [2048], replicated, may hold values from -1.75 to 1.75
- cotangent: bfloat16 [8192, 2048], P('dp'), may hold values from -6 to 6
- prefix: int32 [1], replicated, may hold values from 819 to 4096
- block_order: int32 [32], replicated, may hold values from 0 to 31, as said below
Outputs:
- layer_out: bfloat16 [8192, 2048], P('dp')
- tokens_grad: float32 [8192, 2048], P('dp')
- first_gain_grad: float32 [2048], replicated
- first_shift_grad: float32 [2048], replicated
- query_weight_grad: float32 [2048, 2048], P('dp', 'tensor')
- query_bias_grad: float32 [2048], P('tensor')
- key_weight_grad: float32 [2048, 2048], P('dp', 'tensor')
- value_weight_grad: float32 [2048, 2048], P('dp', 'tensor')
- value_bias_grad: float32 [2048], P('tensor')
- out_weight_grad: float32 [2048, 2048], P('tensor', 'dp')
- out_bias_grad: float32 [2048], replicated
- second_gain_grad: float32 [2048], replicated
- second_shift_grad: float32 [2048], replicated
- up_weight_grad: float32 [2048, 8192], P('dp', 'tensor')
- up_bias_grad: float32 [8192], P('tensor')
- down_weight_grad: float32 [8192, 2048], P('tensor', 'dp')
- down_bias_grad: float32 [2048], replicated
Inputs may be any that keep to these rules, and one draw needn't show every extreme that they name: `block_order`: for each sequence s, entries s * 32 to s * 32 + 31 are a permutation of those same numbers: every stored block lies in its own sequence's rows, but its place within the sequence is shuffled.
All inputs are finite; a program needn't handle non-finite values.
Results may differ from a plain program's by a relative error of at most 0.025.
Values may be sent and summed in bfloat16 or wider, within the bound.
A program may use at most 192 MiB of HBM per device.

v0:
```python
import math
import jax
import jax.numpy as jnp
from jax import lax
from jax.sharding import PartitionSpec as P

HEAD = 128
epsilon = 1e-05
masked_score = -1e30


def sent_together(arrays, axis, dim, along):
    both = jnp.concatenate(arrays, axis=along)
    filled, at, gathered = (lax.all_gather(both, axis, axis=dim, tiled=True), 0, [])
    for a in arrays:
        gathered.append(lax.slice_in_dim(filled, at, at + a.shape[along], axis=along))
        at += a.shape[along]
    return tuple(gathered)


def in_one_piece(arrays, axis, dim, along):
    ends, at = ([], 0)
    for a in arrays[:-1]:
        at += a.shape[along]
        ends.append(at)
    both = jnp.concatenate(arrays, axis=along)
    return tuple(
        jnp.split(lax.psum_scatter(both, axis, scatter_dimension=dim, tiled=True), ends, axis=along)
    )


def from_everyone(value, axis):
    copies = jnp.broadcast_to(value, (lax.axis_size(axis), *value.shape))
    return lax.all_to_all(copies, axis, split_axis=0, concat_axis=0, tiled=True)


def over_copies(value, axis):
    return from_everyone(value, axis).astype(jnp.float32).sum(axis=0)


def to_low(values_in):
    return values_in.astype(jnp.bfloat16)


def matmul(left_side, right_side):
    return jnp.dot(left_side, right_side, preferred_element_type=jnp.float32)


def rows_inner(left_side, right_side):
    return lax.dot_general(
        left_side, right_side, (((0,), (0,)), ((), ())), preferred_element_type=jnp.float32
    )


def cols_inner(left_side, right_side):
    return lax.dot_general(
        left_side, right_side, (((1,), (1,)), ((), ())), preferred_element_type=jnp.float32
    )


def norm_forward(values_in, norm_gain, norm_shift):
    average = jnp.mean(values_in, axis=-1, keepdims=True)
    centred = values_in - average
    variance = jnp.mean(centred * centred, axis=-1, keepdims=True)
    inverse = lax.rsqrt(variance + epsilon)
    scaled = centred * inverse
    return (scaled * norm_gain + norm_shift, scaled, inverse)


def norm_backward(grad_out, scaled, inverse, norm_gain):
    grad_scaled = grad_out * norm_gain
    first_mean = jnp.mean(grad_scaled, axis=-1, keepdims=True)
    second = jnp.mean(grad_scaled * scaled, axis=-1, keepdims=True)
    return inverse * (grad_scaled - first_mean - scaled * second)


def place_of(row_ids, block_order, block_rows, blocks_per_seq):
    blocks = row_ids // block_rows
    table_size = block_order.shape[0]
    matches = blocks[:, None] == jnp.arange(table_size, dtype=jnp.int32)[None, :]
    orders = jnp.sum(jnp.where(matches, block_order[None, :], 0), axis=1)
    return (orders % blocks_per_seq * block_rows + row_ids % block_rows, blocks // blocks_per_seq)


def on_device(
    tokens,
    first_gain,
    first_shift,
    query_weight,
    query_bias,
    key_weight,
    value_weight,
    value_bias,
    out_weight,
    out_bias,
    second_gain,
    second_shift,
    up_weight,
    up_bias,
    down_weight,
    down_bias,
    cotangent,
    prefix,
    block_order,
):
    row_count = tokens.shape[0]
    head_total = query_weight.shape[1] // HEAD
    head_width = head_total * HEAD
    seq_len = row_count * lax.axis_size("dp")
    block_rows = row_count // 2
    blocks_per_seq = seq_len // block_rows
    score_scale = 1.0 / math.sqrt(HEAD)
    dp_index = lax.axis_index("dp")
    own_rows = dp_index * row_count + jnp.arange(row_count, dtype=jnp.int32)
    query_places, query_seqs = place_of(own_rows, block_order, block_rows, blocks_per_seq)
    seq_count = prefix.shape[0]
    seq_match = query_seqs[:, None] == jnp.arange(seq_count, dtype=jnp.int32)[None, :]
    query_limits = jnp.sum(jnp.where(seq_match, prefix[None, :], 0), axis=1)

    def key_mask(first_row, key_width):
        key_rows = first_row + jnp.arange(key_width, dtype=jnp.int32)
        key_places, key_seqs = place_of(key_rows, block_order, block_rows, blocks_per_seq)
        same_seq = key_seqs[None, :] == query_seqs[:, None]
        before = (key_places[None, :] <= query_places[:, None]) | (
            key_places[None, :] < query_limits[:, None]
        )
        return same_seq & before

    rows_gathered = sent_together(
        (to_low(query_weight), to_low(key_weight), to_low(value_weight), to_low(up_weight)),
        "dp",
        0,
        1,
    )
    query_all, key_all, value_all, up_all = rows_gathered
    cols_gathered = sent_together((to_low(out_weight), to_low(down_weight)), "dp", 1, 0)
    out_all, down_all = cols_gathered
    residual = tokens.astype(jnp.float32)
    normed, scaled_one, inverse_one = norm_forward(residual, first_gain, first_shift)
    normed_low = to_low(normed)
    queries = to_low(matmul(normed_low, query_all) + query_bias)
    keys_local = to_low(matmul(normed_low, key_all))
    values_local = to_low(matmul(normed_low, value_all) + value_bias)
    query_heads = queries.reshape(row_count, head_total, HEAD)

    def split_blocks(key_part, value_part):
        part_rows = key_part.shape[0]
        block_width = math.gcd(part_rows, 512)
        block_count = part_rows // block_width
        key_blocks = key_part.reshape(block_count, block_width, head_total, HEAD)
        value_blocks = value_part.reshape(block_count, block_width, head_total, HEAD)
        return (block_width, (key_blocks, value_blocks, jnp.arange(block_count, dtype=jnp.int32)))

    def block_scores(key_block):
        return (
            jnp.einsum("qhd,khd->hqk", query_heads, key_block, preferred_element_type=jnp.float32)
            * score_scale
        )

    key_source, value_source = sent_together((keys_local, values_local), "dp", 0, 1)
    source_start = 0
    block_width, block_items = split_blocks(key_source, value_source)

    def advance(state_now, block_item):
        key_block, value_block, block_index = block_item
        allowed = key_mask(source_start + block_index * block_width, block_width)

        def compute(state_old):
            row_max, row_sum = state_old
            scores = jnp.where(allowed[None], block_scores(key_block), masked_score)
            new_max = jnp.maximum(row_max, jnp.max(scores, axis=-1))
            exponent = jnp.where(allowed[None], jnp.exp(scores - new_max[..., None]), 0.0)
            return (new_max, row_sum * jnp.exp(row_max - new_max) + jnp.sum(exponent, axis=-1))

        return (lax.cond(jnp.any(allowed), compute, lambda state_old: state_old, state_now), None)

    initial = (
        jnp.full((head_total, row_count), masked_score, jnp.float32),
        jnp.zeros((head_total, row_count), jnp.float32),
    )
    running, _ = lax.scan(advance, initial, block_items)
    row_max, row_sum = running
    log_total = row_max + jnp.log(row_sum)
    attention_block_width, block_items = split_blocks(key_source, value_source)

    def advance(weighted, block_item):
        key_block, value_block, block_index = block_item
        allowed = key_mask(
            source_start + block_index * attention_block_width, attention_block_width
        )

        def compute(weighted_old):
            probs = jnp.where(
                allowed[None], jnp.exp(block_scores(key_block) - log_total[..., None]), 0.0
            )
            return weighted_old + jnp.einsum(
                "hqk,khd->hqd", to_low(probs), value_block, preferred_element_type=jnp.float32
            )

        return (
            lax.cond(jnp.any(allowed), compute, lambda weighted_old: weighted_old, weighted),
            None,
        )

    start = jnp.zeros((head_total, row_count, HEAD), jnp.float32)
    weighted, _ = lax.scan(advance, start, block_items)
    mixed_low = to_low(weighted.transpose(1, 0, 2).reshape(row_count, head_width))
    branch = (
        lax.psum(matmul(mixed_low, out_all).astype(jnp.bfloat16), "tensor").astype(jnp.float32)
        + out_bias
    )
    middle = residual + branch
    normed_two, scaled_two, inverse_two = norm_forward(middle, second_gain, second_shift)
    normed_two_low = to_low(normed_two)
    pre_act = matmul(normed_two_low, up_all) + up_bias
    hidden, gelu_back = jax.vjp(lambda inputs: jax.nn.gelu(inputs, approximate=False), pre_act)
    hidden_low = to_low(hidden)
    out_branch = (
        lax.psum(matmul(hidden_low, down_all).astype(jnp.bfloat16), "tensor").astype(jnp.float32)
        + down_bias
    )
    output = middle + out_branch
    grad_out = cotangent.astype(jnp.float32)
    grad_down_bias = jnp.sum(grad_out, axis=0)
    grad_down = rows_inner(hidden_low, cotangent)
    grad_hidden = cols_inner(cotangent, down_all)
    grad_pre_low = to_low(gelu_back(grad_hidden)[0])
    grad_up_bias = jnp.sum(grad_pre_low.astype(jnp.float32), axis=0)
    grad_up = rows_inner(normed_two_low, grad_pre_low)
    grad_normed_two = lax.psum(
        cols_inner(grad_pre_low, up_all).astype(jnp.bfloat16), "tensor"
    ).astype(jnp.float32)
    grad_gain_two = jnp.sum(grad_normed_two * scaled_two, axis=0)
    grad_shift_two = jnp.sum(grad_normed_two, axis=0)
    grad_middle = grad_out + norm_backward(grad_normed_two, scaled_two, inverse_two, second_gain)
    grad_middle_low = to_low(grad_middle)
    grad_out_bias = jnp.sum(grad_middle_low.astype(jnp.float32), axis=0)
    grad_out_weight = rows_inner(mixed_low, grad_middle_low)
    grad_mixed_low = to_low(cols_inner(grad_middle_low, out_all))
    grad_heads = grad_mixed_low.reshape(row_count, head_total, HEAD)
    row_delta = jnp.sum(grad_heads.astype(jnp.float32).transpose(1, 0, 2) * weighted, axis=-1)
    part_rows = key_source.shape[0]
    attend_block_width, block_items = split_blocks(key_source, value_source)

    def advance(grad_query, block_item):
        key_block, value_block, block_index = block_item
        allowed = key_mask(source_start + block_index * attend_block_width, attend_block_width)

        def compute(grad_now):
            probs = jnp.where(
                allowed[None], jnp.exp(block_scores(key_block) - log_total[..., None]), 0.0
            )
            grad_probs = jnp.einsum(
                "qhd,khd->hqk", grad_heads, value_block, preferred_element_type=jnp.float32
            )
            grad_scores = to_low(probs * (grad_probs - row_delta[..., None]))
            new_grad = (
                grad_now
                + jnp.einsum(
                    "hqk,khd->qhd", grad_scores, key_block, preferred_element_type=jnp.float32
                )
                * score_scale
            )
            grad_key = (
                jnp.einsum(
                    "hqk,qhd->khd", grad_scores, query_heads, preferred_element_type=jnp.float32
                )
                * score_scale
            )
            grad_value = jnp.einsum(
                "hqk,qhd->khd", to_low(probs), grad_heads, preferred_element_type=jnp.float32
            )
            return (new_grad, grad_key, grad_value)

        def skipped(grad_now):
            zero_block = jnp.zeros((attend_block_width, head_total, HEAD), jnp.float32)
            return (grad_now, zero_block, zero_block)

        new_grad, grad_key, grad_value = lax.cond(jnp.any(allowed), compute, skipped, grad_query)
        return (new_grad, (grad_key, grad_value))

    start_grad = jnp.zeros((row_count, head_total, HEAD), jnp.float32)
    grad_query, key_terms = lax.scan(advance, start_grad, block_items)
    grad_query, key_term, value_term = (
        grad_query,
        key_terms[0].reshape(part_rows, head_width),
        key_terms[1].reshape(part_rows, head_width),
    )
    grad_keys, grad_values = tuple(
        (
            part.astype(jnp.float32)
            for part in in_one_piece(
                (key_term.astype(jnp.bfloat16), value_term.astype(jnp.bfloat16)), "dp", 0, 1
            )
        )
    )
    grad_query_low = to_low(grad_query.reshape(row_count, head_width))
    grad_keys_low = to_low(grad_keys)
    grad_values_low = to_low(grad_values)
    grad_query_bias = jnp.sum(grad_query_low.astype(jnp.float32), axis=0)
    grad_value_bias = jnp.sum(grad_values_low.astype(jnp.float32), axis=0)
    grad_query_weight = rows_inner(normed_low, grad_query_low)
    grad_key_weight = rows_inner(normed_low, grad_keys_low)
    grad_value_weight = rows_inner(normed_low, grad_values_low)
    local_normed = (
        cols_inner(grad_query_low, query_all)
        + cols_inner(grad_keys_low, key_all)
        + cols_inner(grad_values_low, value_all)
    )
    grad_normed_one = lax.psum(local_normed.astype(jnp.bfloat16), "tensor").astype(jnp.float32)
    grad_gain_one = jnp.sum(grad_normed_one * scaled_one, axis=0)
    grad_shift_one = jnp.sum(grad_normed_one, axis=0)
    grad_tokens = grad_middle + norm_backward(grad_normed_one, scaled_one, inverse_one, first_gain)
    row_sums = tuple(
        (
            part.astype(jnp.float32)
            for part in in_one_piece(
                (
                    grad_query_weight.astype(jnp.bfloat16),
                    grad_key_weight.astype(jnp.bfloat16),
                    grad_value_weight.astype(jnp.bfloat16),
                    grad_up.astype(jnp.bfloat16),
                ),
                "dp",
                0,
                1,
            )
        )
    )
    column_sums = tuple(
        (
            part.astype(jnp.float32)
            for part in in_one_piece(
                (grad_out_weight.astype(jnp.bfloat16), grad_down.astype(jnp.bfloat16)), "dp", 1, 0
            )
        )
    )
    small_sums = (
        over_copies(grad_gain_one.astype(jnp.bfloat16), "dp").astype(jnp.float32),
        over_copies(grad_shift_one.astype(jnp.bfloat16), "dp").astype(jnp.float32),
        over_copies(grad_query_bias.astype(jnp.bfloat16), "dp").astype(jnp.float32),
        over_copies(grad_value_bias.astype(jnp.bfloat16), "dp").astype(jnp.float32),
        over_copies(grad_out_bias.astype(jnp.bfloat16), "dp").astype(jnp.float32),
        over_copies(grad_gain_two.astype(jnp.bfloat16), "dp").astype(jnp.float32),
        over_copies(grad_shift_two.astype(jnp.bfloat16), "dp").astype(jnp.float32),
        over_copies(grad_up_bias.astype(jnp.bfloat16), "dp").astype(jnp.float32),
        over_copies(grad_down_bias.astype(jnp.bfloat16), "dp").astype(jnp.float32),
    )
    return (
        output.astype(jnp.bfloat16),
        grad_tokens,
        small_sums[0],
        small_sums[1],
        row_sums[0],
        small_sums[2],
        row_sums[1],
        row_sums[2],
        small_sums[3],
        column_sums[0],
        small_sums[4],
        small_sums[5],
        small_sums[6],
        row_sums[3],
        small_sums[7],
        column_sums[1],
        small_sums[8],
    )


def solution(mesh):
    return jax.shard_map(
        on_device,
        mesh=mesh,
        in_specs=(
            P("dp", None),
            P(),
            P(),
            P("dp", "tensor"),
            P("tensor"),
            P("dp", "tensor"),
            P("dp", "tensor"),
            P("tensor"),
            P("tensor", "dp"),
            P(),
            P(),
            P(),
            P("dp", "tensor"),
            P("tensor"),
            P("tensor", "dp"),
            P(),
            P("dp", None),
            P(),
            P(),
        ),
        out_specs=(
            P("dp", None),
            P("dp", None),
            P(),
            P(),
            P("dp", "tensor"),
            P("tensor"),
            P("dp", "tensor"),
            P("dp", "tensor"),
            P("tensor"),
            P("tensor", "dp"),
            P(),
            P(),
            P(),
            P("dp", "tensor"),
            P("tensor"),
            P("tensor", "dp"),
            P(),
        ),
        check_vma=False,
    )
```

profile of v0, /device:TPU:3, one launch (start us, length us, event | category | flops | bytes accessed | tf_op | source)
XLA Modules:
  0.0 1173.7 jit_solution(17197489712279023680)
XLA Ops:
  15.4 46.7 %all-gather.4.cloned.1.call-done = bf16[2048,1792]{1,0:T(8,128)(2,1)} async-done(((bf16[128,1792]{1,0:T(8,128)(2,1)}), bf16[2048,1792]{1,0:T(8,128)(2,1)}) %all-gather.4.cloned.1.call-update) | async-done | bytes 7340048 | tf_op jit(solution)/shard_map/all_gather | solution.py:14
  72.3 49.0 %all-gather.6.cloned.1.call-done = bf16[8192,512]{0,1:T(8,128)(2,1)} async-done(((bf16[512,512]{0,1:T(8,128)(2,1)}), bf16[8192,512]{0,1:T(8,128)(2,1)}) %all-gather.6.cloned.1.call-update) | async-done | bytes 8388624 | tf_op jit(solution)/shard_map/all_gather | solution.py:14
  130.2 7.9 copy.143
  138.1 76.3 %while.57 = (s32[]{:T(128)}, f32[2,512]{1,0:T(2,128)S(1)}, f32[2,512]{1,0:T(2,128)S(1)}, s32[16]{0:T(128)S(1)}, s32[32]{0:T(128)S(1)}, /*index=5*/s32[512]{0:T(5...) while((s32[]{:T(128)}, f32[2,512]{1,0:T(2,128)S(1)}, ...), condition=%wide.region_10.11_spmd.clone.clone, body=%wide.region_3.0_spmd.clone.clone.sunk | while | flops 140081152 | bytes 5585795 | solution.py:181
  214.4 6.0 copy.181
  220.4 7.9 copy.145
  228.3 76.4 %while.58 = (s32[]{:T(128)}, f32[2,512,128]{2,1,0:T(8,128)S(1)}, s32[16]{0:T(128)S(1)}, s32[32]{0:T(128)S(1)}, s32[512]{0:T(512)S(1)}, /*index=5*/bf16[16,512,2,...) while((s32[]{:T(128)}, f32[2,512,128]{2,1,0:T(8,128)S(1)}, ...), condition=%wide.region_16.17_spmd.clone.clone, body=%wide.region_11.16_spmd.clone.clone.sunk | while | flops 272330752 | bytes 2391411 | solution.py:206
  309.0 122.2 %all-reduce.5.cloned.1.call-done = bf16[512,2048]{1,0:T(8,128)(2,1)} async-done(((bf16[512,2048]{1,0:T(8,128)(2,1)}), bf16[512,2048]{1,0:T(8,128)(2,1)}) %all-reduce.5.cloned.1.call-update) | async-done | bytes 2097168 | tf_op jit(solution)/shard_map/psum | solution.py:209
  434.8 10.5 multiply_convert_fusion
  453.3 91.3 %all-reduce.7.cloned.1.call-done = bf16[512,2048]{1,0:T(8,128)(2,1)} async-done(((bf16[512,2048]{1,0:T(8,128)(2,1)}), bf16[512,2048]{1,0:T(8,128)(2,1)}) %all-reduce.7.cloned.1.call-update) | async-done | bytes 2097168 | tf_op jit(solution)/shard_map/psum | solution.py:230
  557.1 140.2 %while.59 = (s32[]{:T(128)}, f32[512,2,128]{2,0,1:T(8,128)S(1)}, bf16[16,512,2,128]{3,1,2,0:T(8,128)(2,1)}, bf16[16,512,2,128]{3,1,2,0:T(8,128)(2,1)}, s32[16]{0...) while((s32[]{:T(128)}, f32[512,2,128]{2,0,1:T(8,128)S(1)}, ...), condition=%wide.region_30.31_spmd.clone.clone, body=%wide.region_25.30_spmd.clone.clone.sunk | while | flops 676950016 | bytes 15504335 | solution.py:283
  585.2 5.8 conditional.14
  596.8 5.8 conditional.14
  614.4 5.8 conditional.14
  637.8 5.8 conditional.14
  655.4 5.8 conditional.14
  666.9 5.8 conditional.14
  678.5 5.8 conditional.14
  690.1 5.8 conditional.14
  697.3 7.8 copy.154
  705.2 8.5 copy.183
  713.6 8.0 copy.153
  721.6 8.5 copy.182
  730.1 7.7 pad_maximum_fusion
  745.9 7.9 copy.172
  754.3 6.2 fusion.121
  764.6 118.1 %reduce-scatter.8.cloned.1.call-done = bf16[512,512]{0,1:T(8,128)(2,1)} async-done(((bf16[8192,512]{0,1:T(8,128)(2,1)}), bf16[512,512]{0,1:T(8,128)(2,1)}) %reduce-scatter.8.cloned.1.call-update) | async-done | bytes 524304 | tf_op jit(solution)/shard_map/reduce_scatter | solution.py:28
  899.5 10.1 copy.170
  911.7 6.3 all-to-all-start.7
  985.0 86.7 %all-reduce.9.cloned.1.call-done = (bf16[512,2048]{1,0:T(8,128)(2,1)}, bf16[512,2048]{1,0:T(8,128)(2,1)}) async-done(((bf16[512,2048]{1,0:T(8,128)(2,1)}, bf16[512,2048]{1,0:T(8,128)(2,1)}), (bf16[512,2048]{1,0:T(8,128)(2,1)}, bf16[512,2048]{1,0:T(8,128)(2,1)})) %all-reduce.9.cloned.1.call-update) | async-done | bytes 4194320 | tf_op jit(solution)/shard_map/psum | solution.py:219
  1092.5 7.2 fusion.101
  1101.1 60.2 %reduce-scatter.10.cloned.1.call-done = bf16[128,1792]{1,0:T(8,128)(2,1)} async-done(((bf16[2048,1792]{1,0:T(8,128)(2,1)}), bf16[128,1792]{1,0:T(8,128)(2,1)}) %reduce-scatter.10.cloned.1.call-update) | async-done | bytes 458768
  (719 shorter events, 444.3 us)
Async XLA Ops:
  7.2 54.8 %all-gather.4.cloned.1.call-start = ((), (), s32[]{:S(2)}) async-start(), calls=%async_computation.12 | async-start | bytes 7798784 | tf_op jit(solution)/shard_map/all_gather | solution.py:14
  12.0 109.3 %all-gather.6.cloned.1.call-start = ((), (), s32[]{:S(2)}) async-start(), calls=%async_computation.13 | async-start | bytes 8912896 | tf_op jit(solution)/shard_map/all_gather | solution.py:14
  12.5 49.6 %copy-start.21 = (f32[512]{0:T(512)}, f32[512]{0:T(512)S(1)}, u32[]{:S(2)}) copy-start(f32[512]{0:T(512)S(1)} %broadcast_multiply_fusion.5) | copy-start | bytes 6148
  13.2 51.5 %copy-start.30 = (f32[256]{0:T(256)S(1)}, f32[256]{0:T(256)}, u32[]{:S(2)}) copy-start(f32[256]{0:T(256)} %param.38) | copy-start | bytes 3076
  15.4 52.9 %copy-start.15 = (f32[1024,128]{1,0:T(8,128)S(1)}, f32[1024,128]{1,0:T(8,128)}, u32[]{:S(2)}) copy-start(f32[1024,128]{1,0:T(8,128)} %param.45) | copy-start | bytes 1572868
  15.4 52.9 %copy-start.18 = (f32[256,128]{1,0:T(8,128)S(1)}, f32[256,128]{1,0:T(8,128)}, u32[]{:S(2)}) copy-start(f32[256,128]{1,0:T(8,128)} %param.39) | copy-start | bytes 393220
  68.2 236.8 %all-gather.8.cloned.1.call-start = ((), (), s32[]{:S(2)}) async-start(), calls=%async_computation.14 | async-start | bytes 5570560 | tf_op jit(solution)/shard_map/all_gather | solution.py:14
  69.1 362.1 %all-reduce.5.cloned.1.call-start = ((), (), s32[]{:S(2)}) async-start(), calls=%async_computation.15 | async-start | bytes 4194304 | tf_op jit(solution)/shard_map/psum | solution.py:209
  304.8 128.9 %copy-start.7 = (bf16[512,2,128]{2,0,1:T(8,128)(2,1)}, bf16[512,2,128]{2,0,1:T(8,128)(2,1)S(1)}, u32[]{:S(2)}) copy-start(bf16[512,2,128]{2,0,1:T(8,128)(2,1)S(1)} %get-tuple-element.1875) | copy-start | bytes 786436
  304.8 126.4 %copy-start.16 = (f32[2048]{0:T(1024)S(1)}, f32[2048]{0:T(1024)}, u32[]{:S(2)}) copy-start(f32[2048]{0:T(1024)} %param.40) | copy-start | bytes 24580
  304.9 128.7 %copy-start.11 = (bf16[2,512,128]{1,2,0:T(8,128)(2,1)}, bf16[2,512,128]{1,2,0:T(8,128)(2,1)S(1)}, u32[]{:S(2)}) copy-start(bf16[2,512,128]{1,2,0:T(8,128)(2,1)S(1)} %copy.146) | copy-start | bytes 786436
  308.4 126.4 %copy-start.25 = (f32[2048]{0:T(1024)S(1)}, f32[2048]{0:T(1024)}, u32[]{:S(2)}) copy-start(f32[2048]{0:T(1024)} %param.41) | copy-start | bytes 24580
  308.4 126.4 %copy-start.28 = (f32[2048]{0:T(1024)S(1)}, f32[2048]{0:T(1024)}, u32[]{:S(2)}) copy-start(f32[2048]{0:T(1024)} %param.42) | copy-start | bytes 24580
  308.4 126.4 %copy-start.29 = (f32[1024]{0:T(1024)S(1)}, f32[1024]{0:T(1024)}, u32[]{:S(2)}) copy-start(f32[1024]{0:T(1024)} %param.44) | copy-start | bytes 12292
  308.4 236.2 %all-reduce.7.cloned.1.call-start = ((), (), s32[]{:S(2)}) async-start(), calls=%async_computation.16 | async-start | bytes 4194304 | tf_op jit(solution)/shard_map/psum | solution.py:230
  453.3 429.4 %reduce-scatter.8.cloned.1.call-start = ((), (), s32[]{:S(2)}) async-start(), calls=%async_computation.17 | async-start | bytes 8912896 | tf_op jit(solution)/shard_map/reduce_scatter | solution.py:28
  737.8 242.5 %reduce-scatter.12.cloned.1.call-start = ((), (), s32[]{:S(2)}) async-start(), calls=%async_computation.19 | async-start | bytes 5570560
  753.9 317.8 %all-reduce.9.cloned.1.call-start = ((), (), s32[]{:S(2)}) async-start(), calls=%async_computation.20 | async-start | bytes 8388608 | tf_op jit(solution)/shard_map/psum | solution.py:219
  888.7 272.6 %reduce-scatter.10.cloned.1.call-start = ((), (), s32[]{:S(2)}) async-start(), calls=%async_computation.18 | async-start | bytes 7798784
  909.6 162.1 %copy-start.20 = (f32[2048]{0:T(1024)S(1)}, f32[2048]{0:T(1024)}, u32[]{:S(2)}) copy-start(f32[2048]{0:T(1024)} %param.32) | copy-start | bytes 24580
  909.6 162.1 %copy-start.22 = (f32[512]{0:T(512)S(1)}, f32[512]{0:T(512)}, u32[]{:S(2)}) copy-start(f32[512]{0:T(512)} %copy-done.21) | copy-start | bytes 6148
  909.6 162.1 %copy-start.24 = (f32[512]{0:T(512)S(1)}, f32[512]{0:T(512)}, u32[]{:S(2)}) copy-start(f32[512]{0:T(512)} %copy-done.23) | copy-start | bytes 6148
  911.7 11.0 all-to-all-start.7
  922.7 9.3 all-to-all-start.2
  932.0 9.8 all-to-all-start.4
  941.9 9.9 all-to-all-start.5
  951.8 10.0 all-to-all-start.6
  961.8 9.6 all-to-all-start.8
  974.9 9.6 all-to-all-start.3
  983.1 109.4 %copy-start.27 = (f32[2048]{0:T(1024)S(1)}, f32[2048]{0:T(1024)}, u32[]{:S(2)}) copy-start(f32[2048]{0:T(1024)} %param.46) | copy-start | bytes 24580
  1076.9 10.0 all-to-all-start
  1086.9 12.9 %all-to-all-start.1 = ((bf16[16,2,1024]{2,1,0:T(2,128)(2,1)}), bf16[16,2,1024]{2,1,0:T(2,128)(2,1)S(1)}, u32[]{:S(2)}, u32[]{:S(2)}) async-start(bf16[16,2,1024]{2,1,0:T(2,128)(2,1)} %reshape.433), calls=%async_computation.2 | async-start | bytes 131072 | tf_op jit(solution)/shard_map/all_to_all | solution.py:34
  (30 other events, 215.3 us)
Sparse Core Ops, SparseCore 0:
  12.2 49.8 all-gather.3
  68.3 52.9 all-gather.5
  123.5 50.0 all-gather.7
  308.5 122.6 all-reduce.4
  453.4 91.2 all-reduce.6
  737.9 144.7 reduce-scatter.7
  885.1 69.3 reduce-scatter.11
  957.6 114.0 all-reduce.8
  1074.1 87.1 reduce-scatter.9
where the time goes:
time: 1180 us; the launch traced here: 1170 us
  waiting for transfers between devices  594 us (50%)
  other arithmetic  164 us (14%)
  local copies, waits for them, and re-layouts  153 us (13%)
  matrix products  133 us (11%)
  loops' own time  65.5 us (6%)
  starting transfers between devices  48.9 us (4%)
  between operations  15 us (1%)
    psum x1, waiting for transfers between devices, on_device(): lax.psum(matmul(mixed_low, out_all).astype(jnp.bfloat16), 'tensor')  122 us
    reduce_scatter x1, waiting for transfers between devices, in_one_piece(): lax.psum_scatter(both, axis, scatter_dimension=dim, tiled=True)  118 us
    all_gather x3, waiting for transfers between devices, sent_together(): lax.all_gather(both, axis, axis=dim, tiled=True)  95.7 us
    psum x1, waiting for transfers between devices, on_device(): lax.psum(cols_inner(grad_pre_low, up_all).astype(jnp.bfloat16), 'tensor')  91.3 us
    psum x1, waiting for transfers between devices, on_device(): lax.psum(matmul(hidden_low, down_all).astype(jnp.bfloat16), 'tensor')  86.7 us
    unnamed x111, local copies, waits for them, and re-layouts  74.7 us
    unnamed x11, waiting for transfers between devices  60.3 us
    reduce_or x48, other arithmetic, advance(): jnp.any(allowed)  58 us
  transfers between devices with their start and end apart: 18, of which 15 were waited for; matrix products, arithmetic and copies ran while one was open for 20% of the time, Pallas kernels for 0%

commit v1 on v0

--- a/solution.py
+++ b/solution.py
@@ -1,3 +1,4 @@
+import functools
 import math
 import jax
 import jax.numpy as jnp
@@ -7,6 +8,13 @@
 HEAD = 128
 epsilon = 1e-05
 masked_score = -1e30
+
+
+def _assign_views(u_in, a_name):
+    return lax.all_gather(u_in, axis_name=a_name).sum(axis=0)
+
+
+types_build = functools.partial(_assign_views, a_name="tensor")
 
 
 def sent_together(arrays, axis, dim, along):
@@ -206,8 +214,7 @@
     weighted, _ = lax.scan(advance, start, block_items)
     mixed_low = to_low(weighted.transpose(1, 0, 2).reshape(row_count, head_width))
     branch = (
-        lax.psum(matmul(mixed_low, out_all).astype(jnp.bfloat16), "tensor").astype(jnp.float32)
-        + out_bias
+        types_build(matmul(mixed_low, out_all).astype(jnp.bfloat16)).astype(jnp.float32) + out_bias
     )
     middle = residual + branch
     normed_two, scaled_two, inverse_two = norm_forward(middle, second_gain, second_shift)

time: 1180 us -> 1290 us (1.093)
  waiting for transfers between devices: 594 us -> 689 us
    all_gather x0 -> x1, waiting for transfers between devices: none -> 220 us  [_assign_views(): return lax.all_gather(u_in, axis_name=a_name).sum(axis=0)]
    psum x1 -> x0, waiting for transfers between devices: 122 us -> none  [on_device(): lax.psum(matmul(mixed_low, out_all).astype(jnp.bfloat16), 'tensor')]
  transfers between devices with their start and end apart: 18 -> 18, of which waited for: 15 -> 15; matrix products, arithmetic and copies ran while one was open for 20% -> 19% of each run, Pallas kernels for 0% -> 0%
where the time goes in v1:
time: 1290 us; the launch traced here: 1280 us
  waiting for transfers between devices  689 us (53%)
  other arithmetic  175 us (14%)
  local copies, waits for them, and re-layouts  153 us (12%)
  matrix products  133 us (10%)
  loops' own time  65.5 us (5%)
  starting transfers between devices  47.6 us (4%)
  between operations  14.9 us (1%)
    all_gather x1, waiting for transfers between devices, _assign_views(): return lax.all_gather(u_in, axis_name=a_name).sum(axis=0)  220 us
    reduce_scatter x1, waiting for transfers between devices, in_one_piece(): lax.psum_scatter(both, axis, scatter_dimension=dim, tiled=True)  118 us
    all_gather x3, waiting for transfers between devices, sent_together(): lax.all_gather(both, axis, axis=dim, tiled=True)  95.1 us
    psum x1, waiting for transfers between devices, on_device(): lax.psum(matmul(hidden_low, down_all).astype(jnp.bfloat16), 'tensor')  88.5 us
    psum x1, waiting for transfers between devices, on_device(): lax.psum(cols_inner(grad_pre_low, up_all).astype(jnp.bfloat16), 'tensor')  86.1 us
    unnamed x111, local copies, waits for them, and re-layouts  75.1 us
    unnamed x11, waiting for transfers between devices  60.3 us
    reduce_or x48, other arithmetic, advance(): jnp.any(allowed)  58 us
  transfers between devices with their start and end apart: 18, of which 15 were waited for; matrix products, arithmetic and copies ran while one was open for 19% of the time, Pallas kernels for 0%

profile of v1, /device:TPU:3, one launch (start us, length us, event | category | flops | bytes accessed | tf_op | source)
XLA Modules:
  0.0 1278.7 jit_solution(7326044562958034173)
XLA Ops:
  15.9 46.1 %all-gather.6.cloned.1.call-done = bf16[2048,1792]{1,0:T(8,128)(2,1)} async-done(((bf16[128,1792]{1,0:T(8,128)(2,1)}), bf16[2048,1792]{1,0:T(8,128)(2,1)}) %all-gather.6.cloned.1.call-update) | async-done | bytes 7340048 | tf_op jit(solution)/shard_map/all_gather | solution.py:22
  72.3 49.0 %all-gather.8.cloned.1.call-done = bf16[8192,512]{0,1:T(8,128)(2,1)} async-done(((bf16[512,512]{0,1:T(8,128)(2,1)}), bf16[8192,512]{0,1:T(8,128)(2,1)}) %all-gather.8.cloned.1.call-update) | async-done | bytes 8388624 | tf_op jit(solution)/shard_map/all_gather | solution.py:22
  130.2 7.9 copy.143
  138.1 76.3 %while.57 = (s32[]{:T(128)}, f32[2,512]{1,0:T(2,128)S(1)}, f32[2,512]{1,0:T(2,128)S(1)}, s32[16]{0:T(128)S(1)}, s32[32]{0:T(128)S(1)}, /*index=5*/s32[512]{0:T(5...) while((s32[]{:T(128)}, f32[2,512]{1,0:T(2,128)S(1)}, ...), condition=%wide.region_10.11_spmd.clone.clone, body=%wide.region_3.0_spmd.clone.clone.sunk | while | flops 140081152 | bytes 5585795 | solution.py:189
  214.4 6.0 copy.181
  220.3 7.9 copy.145
  228.3 76.4 %while.58 = (s32[]{:T(128)}, f32[2,512,128]{2,1,0:T(8,128)S(1)}, s32[16]{0:T(128)S(1)}, s32[32]{0:T(128)S(1)}, s32[512]{0:T(512)S(1)}, /*index=5*/bf16[16,512,2,...) while((s32[]{:T(128)}, f32[2,512,128]{2,1,0:T(8,128)S(1)}, ...), condition=%wide.region_16.17_spmd.clone.clone, body=%wide.region_11.16_spmd.clone.clone.sunk | while | flops 272330752 | bytes 2391411 | solution.py:214
  308.3 220.5 %all-gather.12.cloned.1.call-done = bf16[4096,2048]{1,0:T(8,128)(2,1)} async-done(((bf16[512,2048]{1,0:T(8,128)(2,1)}), bf16[4096,2048]{1,0:T(8,128)(2,1)}) %all-gather.12.cloned.1.call-update) | async-done | bytes 16777232 | tf_op jit(solution)/shard_map/all_gather | solution.py:14
  528.7 11.3 reduce_sum.341
  543.7 10.5 multiply_convert_fusion
  562.3 86.1 %all-reduce.4.cloned.1.call-done = bf16[512,2048]{1,0:T(8,128)(2,1)} async-done(((bf16[512,2048]{1,0:T(8,128)(2,1)}), bf16[512,2048]{1,0:T(8,128)(2,1)}) %all-reduce.4.cloned.1.call-update) | async-done | bytes 2097168 | tf_op jit(solution)/shard_map/psum | solution.py:237
  660.9 140.2 %while.59 = (s32[]{:T(128)}, f32[512,2,128]{2,0,1:T(8,128)S(1)}, bf16[16,512,2,128]{3,1,2,0:T(8,128)(2,1)}, bf16[16,512,2,128]{3,1,2,0:T(8,128)(2,1)}, s32[16]{0...) while((s32[]{:T(128)}, f32[512,2,128]{2,0,1:T(8,128)S(1)}, ...), condition=%wide.region_30.31_spmd.clone.clone, body=%wide.region_25.30_spmd.clone.clone.sunk | while | flops 676950016 | bytes 15504335 | solution.py:290
  700.5 5.8 conditional.14
  718.1 5.8 conditional.14
  741.5 5.8 conditional.14
  759.1 5.8 conditional.14
  770.7 5.8 conditional.14
  782.2 5.8 conditional.14
  793.8 5.8 conditional.14
  801.1 7.8 copy.154
  808.9 8.4 copy.183
  817.3 8.0 copy.153
  825.4 8.5 copy.182
  833.8 7.7 pad_maximum_fusion
  849.6 7.8 copy.172
  857.9 6.2 fusion.121
  868.3 118.5 %reduce-scatter.8.cloned.1.call-done = bf16[512,512]{0,1:T(8,128)(2,1)} async-done(((bf16[8192,512]{0,1:T(8,128)(2,1)}), bf16[512,512]{0,1:T(8,128)(2,1)}) %reduce-scatter.8.cloned.1.call-update) | async-done | bytes 524304 | tf_op jit(solution)/shard_map/reduce_scatter | solution.py:36
  1003.5 10.1 copy.170
  1015.7 6.1 all-to-all-start.7
  1088.3 88.5 %all-reduce.6.cloned.1.call-done = (bf16[512,2048]{1,0:T(8,128)(2,1)}, bf16[512,2048]{1,0:T(8,128)(2,1)}) async-done(((bf16[512,2048]{1,0:T(8,128)(2,1)}, bf16[512,2048]{1,0:T(8,128)(2,1)}), (bf16[512,2048]{1,0:T(8,128)(2,1)}, bf16[512,2048]{1,0:T(8,128)(2,1)})) %all-reduce.6.cloned.1.call-update) | async-done | bytes 4194320 | tf_op jit(solution)/shard_map/psum | solution.py:226
  1197.6 7.2 fusion.101
  1206.1 60.2 %reduce-scatter.10.cloned.1.call-done = bf16[128,1792]{1,0:T(8,128)(2,1)} async-done(((bf16[2048,1792]{1,0:T(8,128)(2,1)}), bf16[128,1792]{1,0:T(8,128)(2,1)}) %reduce-scatter.10.cloned.1.call-update) | async-done | bytes 458768
  (720 shorter events, 449.5 us)
Async XLA Ops:
  7.2 54.8 %all-gather.6.cloned.1.call-start = ((), (), s32[]{:S(2)}) async-start(), calls=%async_computation.12 | async-start | bytes 7798784 | tf_op jit(solution)/shard_map/all_gather | solution.py:22
  12.0 109.3 %all-gather.8.cloned.1.call-start = ((), (), s32[]{:S(2)}) async-start(), calls=%async_computation.13 | async-start | bytes 8912896 | tf_op jit(solution)/shard_map/all_gather | solution.py:22
  13.2 51.5 %copy-start.30 = (f32[256]{0:T(256)S(1)}, f32[256]{0:T(256)}, u32[]{:S(2)}) copy-start(f32[256]{0:T(256)} %param.38) | copy-start | bytes 3076
  15.9 52.3 %copy-start.15 = (f32[1024,128]{1,0:T(8,128)S(1)}, f32[1024,128]{1,0:T(8,128)}, u32[]{:S(2)}) copy-start(f32[1024,128]{1,0:T(8,128)} %param.45) | copy-start | bytes 1572868
  15.9 52.3 %copy-start.18 = (f32[256,128]{1,0:T(8,128)S(1)}, f32[256,128]{1,0:T(8,128)}, u32[]{:S(2)}) copy-start(f32[256,128]{1,0:T(8,128)} %param.39) | copy-start | bytes 393220
  68.2 236.7 %all-gather.10.cloned.1.call-start = ((), (), s32[]{:S(2)}) async-start(), calls=%async_computation.14 | async-start | bytes 5570560 | tf_op jit(solution)/shard_map/all_gather | solution.py:22
  69.1 459.7 %all-gather.12.cloned.1.call-start = ((), (), s32[]{:S(2)}) async-start(), calls=%async_computation.17 | async-start | bytes 18874368 | tf_op jit(solution)/shard_map/all_gather | solution.py:14
  304.7 235.4 %copy-start.7 = (bf16[512,2,128]{2,0,1:T(8,128)(2,1)}, bf16[512,2,128]{2,0,1:T(8,128)(2,1)S(1)}, u32[]{:S(2)}) copy-start(bf16[512,2,128]{2,0,1:T(8,128)(2,1)S(1)} %get-tuple-element.1875) | copy-start | bytes 786436
  304.8 235.2 %copy-start.11 = (bf16[2,512,128]{1,2,0:T(8,128)(2,1)}, bf16[2,512,128]{1,2,0:T(8,128)(2,1)S(1)}, u32[]{:S(2)}) copy-start(bf16[2,512,128]{1,2,0:T(8,128)(2,1)S(1)} %copy.146) | copy-start | bytes 786436
  308.2 340.2 %all-reduce.4.cloned.1.call-start = ((), (), s32[]{:S(2)}) async-start(), calls=%async_computation.15 | async-start | bytes 4194304 | tf_op jit(solution)/shard_map/psum | solution.py:237
  528.7 11.3 copy-start.16
  542.6 11.7 slice-start.2
  542.6 15.7 %slice-start = ((s8[7340032]{0:T(1024)(128)(4,1)}), s8[4194304]{0:T(1024)(128)(4,1)S(1)}, s32[]{:S(2)}) async-start(s8[7340032]{0:T(1024)(128)(4,1)} %bitcast.154), calls=%async_computation.21 | async-start | bytes 8388608
  543.7 10.6 copy-start.13
  543.7 14.6 %slice-start.1 = ((s8[7340032]{0:T(1024)(128)(4,1)}), s8[3145728]{0:T(1024)(128)(4,1)S(1)}, s32[]{:S(2)}) async-start(s8[7340032]{0:T(1024)(128)(4,1)} %bitcast.154), calls=%async_computation.22 | async-start | bytes 6291456
  562.3 424.5 %reduce-scatter.8.cloned.1.call-start = ((), (), s32[]{:S(2)}) async-start(), calls=%async_computation.16 | async-start | bytes 8912896 | tf_op jit(solution)/shard_map/reduce_scatter | solution.py:36
  841.5 242.0 %reduce-scatter.12.cloned.1.call-start = ((), (), s32[]{:S(2)}) async-start(), calls=%async_computation.19 | async-start | bytes 5570560
  857.5 319.3 %all-reduce.6.cloned.1.call-start = ((), (), s32[]{:S(2)}) async-start(), calls=%async_computation.20 | async-start | bytes 8388608 | tf_op jit(solution)/shard_map/psum | solution.py:226
  992.8 273.6 %reduce-scatter.10.cloned.1.call-start = ((), (), s32[]{:S(2)}) async-start(), calls=%async_computation.18 | async-start | bytes 7798784
  1013.6 163.1 %copy-start.20 = (f32[2048]{0:T(1024)S(1)}, f32[2048]{0:T(1024)}, u32[]{:S(2)}) copy-start(f32[2048]{0:T(1024)} %param.32) | copy-start | bytes 24580
  1013.6 163.1 %copy-start.22 = (f32[512]{0:T(512)S(1)}, f32[512]{0:T(512)}, u32[]{:S(2)}) copy-start(f32[512]{0:T(512)} %copy-done.21) | copy-start | bytes 6148
  1013.7 163.1 %copy-start.24 = (f32[512]{0:T(512)S(1)}, f32[512]{0:T(512)}, u32[]{:S(2)}) copy-start(f32[512]{0:T(512)} %copy-done.23) | copy-start | bytes 6148
  1015.7 10.8 all-to-all-start.7
  1026.5 9.2 all-to-all-start.2
  1035.7 9.9 all-to-all-start.4
  1045.6 9.8 all-to-all-start.5
  1055.4 9.7 all-to-all-start.6
  1065.0 9.6 all-to-all-start.8
  1078.1 9.6 all-to-all-start.3
  1086.3 111.2 %copy-start.27 = (f32[2048]{0:T(1024)S(1)}, f32[2048]{0:T(1024)}, u32[]{:S(2)}) copy-start(f32[2048]{0:T(1024)} %param.46) | copy-start | bytes 24580
  1181.9 10.0 all-to-all-start
  1191.9 12.9 %all-to-all-start.1 = ((bf16[16,2,1024]{2,1,0:T(2,128)(2,1)}), bf16[16,2,1024]{2,1,0:T(2,128)(2,1)S(1)}, u32[]{:S(2)}, u32[]{:S(2)}) async-start(bf16[16,2,1024]{2,1,0:T(2,128)(2,1)} %reshape.434), calls=%async_computation.2 | async-start | bytes 131072 | tf_op jit(solution)/shard_map/all_to_all | solution.py:42
  (30 other events, 127.0 us)
Sparse Core Ops, SparseCore 0:
  12.2 49.8 all-gather.5
  68.3 52.9 all-gather.7
  123.5 49.9 all-gather.9
  308.3 220.3 all-gather.11
  562.4 85.9 all-reduce.3
  841.7 145.0 reduce-scatter.7
  989.1 68.3 reduce-scatter.11
  1060.6 116.0 all-reduce.5
  1179.1 87.1 reduce-scatter.9
